TPU v7x, 512 devices: a whole 4x4x16 slice. The times are simulated.
512 devices in a mesh: row: 32 (over y, z_hi, core), col: 16 (over z_lo, x).
Axes of the slice: x: 4, y: 4, z: 16 (z_hi: 4, z_lo: 4; z = z_hi * 4 + z_lo), core: 2. Of those that a mesh axis runs over, the one named last changes fastest.
Arguments:
- forcing_terms: float32 [32, 16, 2, 32, 128], P('row', 'col'), may hold values from -6 to 6
- diagonal_reciprocal: float32 [32, 16, 2, 128, 128], P('row', 'col'), may hold values from -0.5 to 0.5
- stiffness_submatrix: float32 [32, 16, 32, 128, 128], P('row', 'col'), may hold values from -0.1875 to 0.1875
- stiffness_source_index: int32 [32, 16, 32], P('row', 'col'), may hold values from 0 to 31
- stiffness_target_index: int32 [32, 16, 32], P('row', 'col'), may hold values from 0 to 63
- stiffness_nonzero_tally: int32 [32, 16], P('row', 'col'), may hold values from 1 to 32, as said below
- interpolant_submatrix: float32 [32, 16, 16, 128, 128], P('row', 'col'), may hold values from -0.0625 to 0.0625
- interpolant_cluster_index: int32 [32, 16, 16], P('row', 'col'), may hold values from 0 to 1
- interpolant_target_index: int32 [32, 16, 16], P('row', 'col'), may hold values from 0 to 63
- interpolant_nonzero_tally: int32 [32, 16], P('row', 'col'), may hold values from 1 to 16, as said below
- provisional_interpolant: float32 [32, 16, 2, 128], P('row', 'col'), may hold values from 0.2 to 1
- cluster_label: int32 [32, 16, 2, 128], P('row', 'col'), may hold values from 0 to 255
Outputs:
- relaxed_iterate: float32 [32, 16, 2, 32, 128], P('row', 'col')
- residual: float32 [32, 16, 2, 32, 128], P('row', 'col')
- coarse: float32 [32, 2, 32, 128], P('row')
Inputs may be any that keep to these rules, and one draw needn't show every extreme that they name: `stiffness_nonzero_tally`: tile slots at or past the count are unused; some pair has all 32 slots live in every draw. `interpolant_nonzero_tally`: tile slots at or past the count are unused; some pair has all 16 slots live in every draw.
All inputs are finite; a program needn't handle non-finite values.
Results may differ from a plain program's by a relative error of at most 0.0003.
Values sent between devices are 32-bit elements; how exact they have to be, the bound alone decides.
No kernel may reach another device: no remote copies, remote signals or barrier semaphores. Data moves between devices by JAX's collectives and lax.ppermute only.
A program may use at most 64 MiB of HBM per device.

v0:
```python
import jax
import jax.numpy as jnp
from jax import lax
from jax.experimental import pallas as pl
from jax.experimental.pallas import tpu as pltpu
from jax.sharding import Mesh, PartitionSpec as P


omega = 0.7
unroll = 16
grant = 16 * 2**20
f32 = jnp.float32
bf16 = jnp.bfloat16


def split(v):
    high = v.astype(bf16)
    return high, (v - high.astype(f32)).astype(bf16)


def product(x, w):
    n, m = x.shape[0], w.shape[1]
    left = jnp.concatenate(split(x), axis=0)
    right = jnp.concatenate(split(w), axis=1)
    full = jnp.dot(left, right, preferred_element_type=f32)
    small = full[:n, m:] + full[n:, :m] + full[n:, m:]
    return full[:n, :m] + small


def first_kernel(source_in, inverse_in, first, source, inverse, done):
    arrivals = [
        pltpu.make_async_copy(inverse_in, inverse, done.at[0]),
        pltpu.make_async_copy(source_in, source, done.at[1]),
    ]
    for arrival in arrivals:
        arrival.start()
    for arrival in arrivals:
        arrival.wait()
    for p in range(source.shape[0]):
        first[p] = omega * product(source[p], inverse[p])


def column_sum(parts, p):
    total = parts[0, p]
    for j in range(1, parts.shape[0]):
        total = total + parts[j, p]
    return total


def relax_kernel(source, inverse, first, parts, relaxed):
    for p in range(source.shape[0]):
        image = column_sum(parts, p)
        relaxed[p] = first[p] + omega * product(source[p] - image, inverse[p])


def residual_kernel(source, parts, weights, labels, residual, tentative):
    pblocks, nrhs, width = source.shape
    total = jnp.zeros((nrhs, pblocks * width), f32)
    for p in range(pblocks):
        value = source[p] - column_sum(parts, p)
        residual[p] = value
        weighted = value * weights[p : p + 1, :]
        aggregate = lax.broadcasted_iota(jnp.int32, (pblocks * width, width), 0)
        member = (aggregate == labels[p : p + 1, :]).astype(f32).astype(bf16)
        high, rest = split(weighted)
        low = (weighted - high.astype(f32) - rest.astype(f32)).astype(bf16)
        stacked = jnp.concatenate([high, rest, low, low], axis=0)
        spreadsum = lax.dot_general(
            stacked, member, (((1,), (1,)), ((), ())), preferred_element_type=f32
        )
        total = total + (
            spreadsum[:nrhs]
            + (spreadsum[nrhs : 2 * nrhs] + spreadsum[2 * nrhs : 3 * nrhs])
        )
    for p in range(pblocks):
        tentative[p] = total[:, p * width : (p + 1) * width]


def sum_kernel(parts, out):
    for p in range(out.shape[0]):
        out[p] = column_sum(parts, p)


def save_kernel(value, out):
    out[...] = value[...]


def tile_kernel(core, count, rows, cols, own, other, tiles, start, out):
    nout = out.shape[0]
    nsource = own.shape[0]
    live_count = count[0]
    mine = core[0]
    if start is None:
        out[...] = jnp.zeros_like(out)
    else:
        out[...] = start[...]

    def group(g, carry):
        terms = []
        for u in range(unroll):
            slot = g * unroll + u
            live = slot < live_count
            target = jnp.clip(cols[slot], 0, 2 * nsource - 1)
            index = (target // 4) * 2 + target % 2
            same = (target // 2) % 2 == mine
            x = jnp.where(same, own[index], other[index])
            x = jnp.where(live, x, 0.0)
            terms.append((jnp.clip(rows[slot], 0, nout - 1), product(x, tiles[slot])))
        for row, term in terms:
            out[row] = out[row] + term
        return carry

    lax.fori_loop(0, (live_count + unroll - 1) // unroll, group, 0)


def vmem(n):
    return [pl.BlockSpec(memory_space=pltpu.VMEM)] * n


def smem(n):
    return [pl.BlockSpec(memory_space=pltpu.SMEM)] * n


def call(kernel, shapes, *args):
    return pl.pallas_call(
        kernel,
        out_shape=tuple(jax.ShapeDtypeStruct(s, f32) for s in shapes),
        in_specs=vmem(len(args)),
        out_specs=tuple(vmem(len(shapes))),
        compiler_params=pltpu.CompilerParams(vmem_limit_bytes=grant),
    )(*args)


def tile_terms(core, count, rows, cols, own, other, tiles, start, nout):
    block = own.shape[1:]
    extra = () if start is None else (start,)

    def kernel(core, count, rows, cols, own, other, tiles, *rest):
        tile_kernel(core, count, rows, cols, own, other, tiles,
                    None if start is None else rest[0], rest[-1])

    return pl.pallas_call(
        kernel,
        out_shape=jax.ShapeDtypeStruct((nout,) + block, f32),
        in_specs=smem(4) + vmem(3 + len(extra)),
        out_specs=pl.BlockSpec(memory_space=pltpu.VMEM),
        compiler_params=pltpu.CompilerParams(vmem_limit_bytes=grant),
    )(core, count, rows, cols, own, other, tiles, *extra)


def pairs(v, axis):
    v = lax.all_gather(v, axis, axis=0, tiled=True, axis_index_groups=[[0, 1], [2, 3]])
    v = lax.optimization_barrier(v)
    return lax.all_gather(v, axis, axis=0, tiled=True, axis_index_groups=[[1, 2], [0, 3]])


def fan(v, axis):
    n = lax.axis_size(axis)
    v = lax.optimization_barrier(jnp.broadcast_to(v[None], (n,) + v.shape))
    return lax.all_to_all(v, axis, 0, 0, tiled=True)


def gather_rows(value):
    block = value.shape
    planes = fan(pairs(value[None], "zh"), "y")
    own = lax.optimization_barrier(planes.reshape((-1,) + block[1:]))
    other = lax.ppermute(own, "core", [(0, 1), (1, 0)])
    return own, other


def sum_columns(partial, pblocks):
    chunks = partial.reshape((-1, pblocks) + partial.shape[1:])
    return lax.all_to_all(chunks, ("zl", "x"), 0, 0, tiled=True)


def body(
    forcing_terms,
    diagonal_reciprocal,
    stiffness_submatrix,
    stiffness_source_index,
    stiffness_target_index,
    stiffness_nonzero_tally,
    interpolant_submatrix,
    interpolant_cluster_index,
    interpolant_target_index,
    interpolant_nonzero_tally,
    provisional_interpolant,
    cluster_label,
):
    source = forcing_terms[0, 0]
    inverse = diagonal_reciprocal[0, 0]
    tiles = stiffness_submatrix[0, 0]
    rows = stiffness_source_index[0, 0]
    cols = stiffness_target_index[0, 0]
    count = stiffness_nonzero_tally[0]
    core = lax.axis_index("core").astype(jnp.int32).reshape(1)
    pblocks = source.shape[0]
    ncol = lax.axis_size(("zl", "x"))
    block = source.shape

    first = pl.pallas_call(
        first_kernel,
        out_shape=jax.ShapeDtypeStruct(block, f32),
        in_specs=[pl.BlockSpec(memory_space=pltpu.MemorySpace.HBM)] * 2,
        out_specs=pl.BlockSpec(memory_space=pltpu.VMEM),
        scratch_shapes=[
            pltpu.VMEM(block, f32),
            pltpu.VMEM(inverse.shape, f32),
            pltpu.SemaphoreType.DMA((2,)),
        ],
        compiler_params=pltpu.CompilerParams(vmem_limit_bytes=grant),
        name="first",
    )(
        pltpu.with_memory_space_constraint(source, pltpu.MemorySpace.HBM),
        pltpu.with_memory_space_constraint(inverse, pltpu.MemorySpace.HBM),
    )
    own, other = gather_rows(first)
    partial = tile_terms(core, count, rows, cols, own, other, tiles, None, ncol * pblocks)
    parts = sum_columns(partial, pblocks)
    (relaxed,) = call(relax_kernel, (block,), source, inverse, first, parts)
    own, other = gather_rows(relaxed)
    partial = tile_terms(core, count, rows, cols, own, other, tiles, None, ncol * pblocks)
    parts = sum_columns(partial, pblocks)
    residual, tentative = call(
        residual_kernel,
        (block, block),
        source,
        parts,
        provisional_interpolant[0, 0],
        cluster_label[0, 0],
    )
    own, other = gather_rows(residual)
    share = tile_terms(
        core,
        interpolant_nonzero_tally[0],
        interpolant_cluster_index[0, 0],
        interpolant_target_index[0, 0],
        own,
        other,
        interpolant_submatrix[0, 0],
        tentative,
        pblocks,
    )
    shares = fan(share, "x")
    (share,) = call(sum_kernel, (block,), shares)
    shares = fan(share, "zl")
    (coarse,) = call(sum_kernel, (block,), shares)
    (relaxed,) = call(save_kernel, (block,), relaxed)
    (residual,) = call(save_kernel, (block,), residual)
    return (relaxed[None, None], residual[None, None], coarse[None])


def solution(mesh):
    grid = Mesh(mesh.devices.reshape(4, 4, 2, 4, 4), ("y", "zh", "core", "zl", "x"))
    row = ("y", "zh", "core")
    col = ("zl", "x")
    spec = P(row, col)

    return jax.shard_map(
        body,
        mesh=grid,
        in_specs=(spec,) * 12,
        out_specs=(spec, spec, P(row)),
        check_vma=False,
    )
```

profile of v0, /device:TPU:24, one launch (start us, length us, event | category | flops | bytes accessed | tf_op | source)
XLA Modules:
  0.0 173.2 jit_solution(2362843611533819335)
XLA Ops:
  0.6 0.0 copy-start.4
  0.6 0.0 copy-start.5
  0.7 0.0 copy-start
  0.7 1.2 first.1
  1.9 9.7 %all-gather = f32[4,32,128]{2,1,0:T(8,128)S(1)} all-gather(f32[2,32,128]{2,1,0:T(8,128)S(1)} %first.1), channel_id=2, replica_groups={{0,32},{64,96},{1,33},{65,97},{2,34},{66,98},{3,35},{67,99},{4,36},{68,..., dimensions={0}, use_global_device_ids=true | all-gather | bytes 98304 | tf_op jit(solution)/shard_map/all_gather | solution.py:152
  11.6 14.0 %all_gather.19 = f32[4,2,32,128]{3,2,1,0:T(8,128)S(1)} all-gather(f32[2,2,32,128]{3,2,1,0:T(8,128)S(1)} %bitcast.51), channel_id=1, replica_groups={{32,64},{0,96},{33,65},{1,97},{34,66},{2,98},{35,67},{3,99},{36,68},{4,..., dimensions={0}, use_global_device_ids=true | all-gather | bytes 196608 | tf_op jit(solution)/shard_map/all_gather | solution.py:154
  25.7 10.5 %all_to_all.35 = f32[4,4,2,32,128]{4,3,2,1,0:T(8,128)S(1)} all-to-all(f32[4,4,2,32,128]{4,3,2,1,0:T(8,128)S(1)} %broadcast_in_dim.23), channel_id=1, replica_groups=mesh['y'=4,'zh'=4,'core'=2,'zl'=4,'x'=4] {'y'}, dimensions={0} | all-to-all | bytes 1048576 | tf_op jit(solution)/shard_map/all_to_all | solution.py:160
  36.2 1.9 %collective-permute-start = (f32[32,32,128]{2,1,0:T(8,128)S(1)}, f32[32,32,128]{2,1,0:T(8,128)S(1)}, u32[]{:S(2)}, u32[]{:S(2)}) collective-permute-start(f32[32,32,128]{2,1,0:T(8,128)S(1)} %bitcast.29), channel_id=1, source_target_pairs={{0,16},{16,0},{1,17},{17,1},{2,18},{18,2},{3,19},{19,3},{4,20},{20... | collective-permute-start | bytes 1572872 | tf_op jit(solution)/shard_map/ppermute | solution.py:167
  38.8 1.2 collective-permute-done.other
  40.0 0.0 copy-done.4
  40.0 0.0 copy-done.5
  40.0 0.0 copy-done
  40.0 0.0 copy-start.2
  40.0 0.0 copy-start.3
  40.0 1.4 shard_map.139
  41.4 23.3 %all_to_all.36.parts = f32[16,2,32,128]{3,2,1,0:T(8,128)S(1)} all-to-all(f32[16,2,32,128]{3,2,1,0:T(8,128)S(1)} %bitcast.36), channel_id=1, replica_groups=mesh['y'=4,'zh'=4,'core'=2,'zl'=4,'x'=4] {'zl','x'}, dimensions={0} | all-to-all | bytes 1048576 | tf_op jit(solution)/shard_map/all_to_all | solution.py:173
  64.7 0.0 copy-done.2
  64.7 0.0 copy-done.3
  64.7 0.2 shard_map.140.value
  64.9 8.6 %all-gather.1 = f32[4,32,128]{2,1,0:T(8,128)S(1)} all-gather(f32[2,32,128]{2,1,0:T(8,128)S(1)} %shard_map.140.value), channel_id=3, replica_groups={{0,32},{64,96},{1,33},{65,97},{2,34},{66,98},{3,35},{67,99},{4,36},{68,..., dimensions={0}, use_global_device_ids=true | all-gather | bytes 98304 | tf_op jit(solution)/shard_map/all_gather | solution.py:152
  73.5 9.0 %all_gather.21 = f32[4,2,32,128]{3,2,1,0:T(8,128)S(1)} all-gather(f32[2,2,32,128]{3,2,1,0:T(8,128)S(1)} %bitcast.52), channel_id=1, replica_groups={{32,64},{0,96},{33,65},{1,97},{34,66},{2,98},{35,67},{3,99},{36,68},{4,..., dimensions={0}, use_global_device_ids=true | all-gather | bytes 196608 | tf_op jit(solution)/shard_map/all_gather | solution.py:154
  82.6 10.5 %all_to_all.37 = f32[4,4,2,32,128]{4,3,2,1,0:T(8,128)S(1)} all-to-all(f32[4,4,2,32,128]{4,3,2,1,0:T(8,128)S(1)} %broadcast_in_dim.52), channel_id=1, replica_groups=mesh['y'=4,'zh'=4,'core'=2,'zl'=4,'x'=4] {'y'}, dimensions={0} | all-to-all | bytes 1048576 | tf_op jit(solution)/shard_map/all_to_all | solution.py:160
  93.1 1.9 %collective-permute-start.1 = (f32[32,32,128]{2,1,0:T(8,128)S(1)}, f32[32,32,128]{2,1,0:T(8,128)S(1)}, u32[]{:S(2)}, u32[]{:S(2)}) collective-permute-start(f32[32,32,128]{2,1,0:T(8,128)S(1)} %bitcast.33), channel_id=1, source_target_pairs={{0,16},{16,0},{1,17},{17,1},{2,18},{18,2},{3,19},{19,3},{4,20},{20... | collective-permute-start | bytes 1572872 | tf_op jit(solution)/shard_map/ppermute | solution.py:167
  95.0 1.9 %collective-permute-done.1.other = f32[32,32,128]{2,1,0:T(8,128)S(1)} collective-permute-done((f32[32,32,128]{2,1,0:T(8,128)S(1)}, f32[32,32,128]{2,1,0:T(8,128)S(1)}, u32[]{:S(2)}, u32[]{:S(2)}) %collective-permute-start.1) | collective-permute-done | bytes 524320 | tf_op jit(solution)/shard_map/ppermute | solution.py:167
  96.9 0.0 copy-start.6
  96.9 0.0 copy-start.7
  96.9 1.4 shard_map.142
  98.3 0.0 copy-start.1
  98.3 0.0 copy-start.8
  98.3 0.0 copy-start.9
  98.3 21.1 %all_to_all.38.parts = f32[16,2,32,128]{3,2,1,0:T(8,128)S(1)} all-to-all(f32[16,2,32,128]{3,2,1,0:T(8,128)S(1)} %bitcast.35), channel_id=1, replica_groups=mesh['y'=4,'zh'=4,'core'=2,'zl'=4,'x'=4] {'zl','x'}, dimensions={0} | all-to-all | bytes 1048576 | tf_op jit(solution)/shard_map/all_to_all | solution.py:173
  119.4 0.0 copy-done.6
  119.4 0.0 copy-done.7
  119.4 0.2 shard_map.143
  119.6 8.6 %all-gather.2 = f32[4,32,128]{2,1,0:T(8,128)S(1)} all-gather(f32[2,32,128]{2,1,0:T(8,128)S(1)} %get-tuple-element.5.value), channel_id=4, replica_groups={{0,32},{64,96},{1,33},{65,97},{2,34},{66,98},{3,35},{67,99},{4,36},{68,..., dimensions={0}, use_global_device_ids=true | all-gather | bytes 98304 | tf_op jit(solution)/shard_map/all_gather | solution.py:152
  128.3 9.0 %all_gather.23 = f32[4,2,32,128]{3,2,1,0:T(8,128)S(1)} all-gather(f32[2,2,32,128]{3,2,1,0:T(8,128)S(1)} %bitcast.53), channel_id=1, replica_groups={{32,64},{0,96},{33,65},{1,97},{34,66},{2,98},{35,67},{3,99},{36,68},{4,..., dimensions={0}, use_global_device_ids=true | all-gather | bytes 196608 | tf_op jit(solution)/shard_map/all_gather | solution.py:154
  137.3 10.5 %all_to_all.39 = f32[4,4,2,32,128]{4,3,2,1,0:T(8,128)S(1)} all-to-all(f32[4,4,2,32,128]{4,3,2,1,0:T(8,128)S(1)} %broadcast_in_dim.55), channel_id=1, replica_groups=mesh['y'=4,'zh'=4,'core'=2,'zl'=4,'x'=4] {'y'}, dimensions={0} | all-to-all | bytes 1048576 | tf_op jit(solution)/shard_map/all_to_all | solution.py:160
  147.8 1.9 %collective-permute-start.2 = (f32[32,32,128]{2,1,0:T(8,128)S(1)}, f32[32,32,128]{2,1,0:T(8,128)S(1)}, u32[]{:S(2)}, u32[]{:S(2)}) collective-permute-start(f32[32,32,128]{2,1,0:T(8,128)S(1)} %bitcast.31), channel_id=1, source_target_pairs={{0,16},{16,0},{1,17},{17,1},{2,18},{18,2},{3,19},{19,3},{4,20},{20... | collective-permute-start | bytes 1572872 | tf_op jit(solution)/shard_map/ppermute | solution.py:167
  150.4 1.2 collective-permute-done.2.other
  151.6 0.0 copy-done.1
  151.6 0.0 copy-done.8
  151.6 0.0 copy-done.9
  151.6 1.0 shard_map.145
  152.6 8.7 %all_to_all.40.parts = f32[4,2,32,128]{3,2,1,0:T(8,128)S(1)} all-to-all(f32[4,2,32,128]{3,2,1,0:T(8,128)S(1)} %broadcast_in_dim.56), channel_id=1, replica_groups=mesh['y'=4,'zh'=4,'core'=2,'zl'=4,'x'=4] {'x'}, dimensions={0} | all-to-all | bytes 262144 | tf_op jit(solution)/shard_map/all_to_all | solution.py:160
  161.3 0.7 broadcast_in_dim.57
  162.0 4.7 %all-to-all-start.6 = ((f32[4,2,32,128]{3,2,1,0:T(8,128)}), f32[4,2,32,128]{3,2,1,0:T(8,128)S(1)}, u32[]{:S(2)}, u32[]{:S(2)}) async-start(f32[4,2,32,128]{3,2,1,0:T(8,128)} %broadcast_in_dim.57), calls=%async_computation.6 | async-start | bytes 262144 | tf_op jit(solution)/shard_map/all_to_all | solution.py:160
  166.7 0.6 shard_map.141
  167.3 0.6 shard_map.144
  167.9 4.7 %all-to-all-done.6.parts = f32[4,2,32,128]{3,2,1,0:T(8,128)S(1)} async-done(((f32[4,2,32,128]{3,2,1,0:T(8,128)}), f32[4,2,32,128]{3,2,1,0:T(8,128)S(1)}, u32[]{:S(2)}, u32[]{:S(2)}) %all-to-all-start.6) | async-done | bytes 131104 | tf_op jit(solution)/shard_map/all_to_all | solution.py:160
  172.6 0.6 shard_map.147
  (5 shorter events, 0.2 us)
Async XLA Ops:
  0.6 39.4 %copy-start.4 = (s32[1,1,32]{2,1,0:T(1,128)S(1)}, s32[1,1,32]{2,1,0:T(1,128)}, u32[]{:S(2)}) copy-start(s32[1,1,32]{2,1,0:T(1,128)} %param.15) | copy-start | bytes 388
  0.6 39.3 %copy-start.5 = (s32[1,1,32]{2,1,0:T(1,128)S(1)}, s32[1,1,32]{2,1,0:T(1,128)}, u32[]{:S(2)}) copy-start(s32[1,1,32]{2,1,0:T(1,128)} %param.16) | copy-start | bytes 388
  0.7 39.3 %copy-start = (f32[1,1,32,128,128]{4,3,2,1,0:T(8,128)S(1)}, f32[1,1,32,128,128]{4,3,2,1,0:T(8,128)}, u32[]{:S(2)}) copy-start(f32[1,1,32,128,128]{4,3,2,1,0:T(8,128)} %param.14) | copy-start | bytes 6291460
  36.2 3.8 %collective-permute-start = (f32[32,32,128]{2,1,0:T(8,128)S(1)}, f32[32,32,128]{2,1,0:T(8,128)S(1)}, u32[]{:S(2)}, u32[]{:S(2)}) collective-permute-start(f32[32,32,128]{2,1,0:T(8,128)S(1)} %bitcast.29), channel_id=1, source_target_pairs={{0,16},{16,0},{1,17},{17,1},{2,18},{18,2},{3,19},{19,3},{4,20},{20... | collective-permute-start | bytes 1572872 | tf_op jit(solution)/shard_map/ppermute | solution.py:167
  40.0 24.7 %copy-start.2 = (f32[1,1,2,128,128]{4,3,2,1,0:T(8,128)S(1)}, f32[1,1,2,128,128]{4,3,2,1,0:T(8,128)}, u32[]{:S(2)}) copy-start(f32[1,1,2,128,128]{4,3,2,1,0:T(8,128)} %param.13) | copy-start | bytes 393220
  40.0 24.7 %copy-start.3 = (f32[1,1,2,32,128]{4,3,2,1,0:T(8,128)S(1)}, f32[1,1,2,32,128]{4,3,2,1,0:T(8,128)}, u32[]{:S(2)}) copy-start(f32[1,1,2,32,128]{4,3,2,1,0:T(8,128)} %param.12) | copy-start | bytes 98308
  93.1 3.8 %collective-permute-start.1 = (f32[32,32,128]{2,1,0:T(8,128)S(1)}, f32[32,32,128]{2,1,0:T(8,128)S(1)}, u32[]{:S(2)}, u32[]{:S(2)}) collective-permute-start(f32[32,32,128]{2,1,0:T(8,128)S(1)} %bitcast.33), channel_id=1, source_target_pairs={{0,16},{16,0},{1,17},{17,1},{2,18},{18,2},{3,19},{19,3},{4,20},{20... | collective-permute-start | bytes 1572872 | tf_op jit(solution)/shard_map/ppermute | solution.py:167
  96.9 22.5 %copy-start.6 = (f32[1,1,2,128]{3,2,1,0:T(2,128)S(1)}, f32[1,1,2,128]{3,2,1,0:T(2,128)}, u32[]{:S(2)}) copy-start(f32[1,1,2,128]{3,2,1,0:T(2,128)} %param.22) | copy-start | bytes 3076
  96.9 22.5 %copy-start.7 = (s32[1,1,2,128]{3,2,1,0:T(2,128)S(1)}, s32[1,1,2,128]{3,2,1,0:T(2,128)}, u32[]{:S(2)}) copy-start(s32[1,1,2,128]{3,2,1,0:T(2,128)} %param.23) | copy-start | bytes 3076
  98.3 53.3 %copy-start.1 = (f32[1,1,16,128,128]{4,3,2,1,0:T(8,128)S(1)}, f32[1,1,16,128,128]{4,3,2,1,0:T(8,128)}, u32[]{:S(2)}) copy-start(f32[1,1,16,128,128]{4,3,2,1,0:T(8,128)} %param.18) | copy-start | bytes 3145732
  98.3 53.3 %copy-start.8 = (s32[1,1,16]{2,1,0:T(1,128)S(1)}, s32[1,1,16]{2,1,0:T(1,128)}, u32[]{:S(2)}) copy-start(s32[1,1,16]{2,1,0:T(1,128)} %param.19) | copy-start | bytes 196
  98.3 53.3 %copy-start.9 = (s32[1,1,16]{2,1,0:T(1,128)S(1)}, s32[1,1,16]{2,1,0:T(1,128)}, u32[]{:S(2)}) copy-start(s32[1,1,16]{2,1,0:T(1,128)} %param.20) | copy-start | bytes 196
  147.8 3.8 %collective-permute-start.2 = (f32[32,32,128]{2,1,0:T(8,128)S(1)}, f32[32,32,128]{2,1,0:T(8,128)S(1)}, u32[]{:S(2)}, u32[]{:S(2)}) collective-permute-start(f32[32,32,128]{2,1,0:T(8,128)S(1)} %bitcast.31), channel_id=1, source_target_pairs={{0,16},{16,0},{1,17},{17,1},{2,18},{18,2},{3,19},{19,3},{4,20},{20... | collective-permute-start | bytes 1572872 | tf_op jit(solution)/shard_map/ppermute | solution.py:167
  162.0 10.6 %all-to-all-start.6 = ((f32[4,2,32,128]{3,2,1,0:T(8,128)}), f32[4,2,32,128]{3,2,1,0:T(8,128)S(1)}, u32[]{:S(2)}, u32[]{:S(2)}) async-start(f32[4,2,32,128]{3,2,1,0:T(8,128)} %broadcast_in_dim.57), calls=%async_computation.6 | async-start | bytes 262144 | tf_op jit(solution)/shard_map/all_to_all | solution.py:160
where the time goes:
time: 175 us; the launch traced here: 173 us
  blocking collectives  144 us (82%)
  starting transfers between devices  10.4 us (6%)
  waiting for transfers between devices  9.01 us (5%)
  Pallas kernels  7.26 us (4%)
  between operations  2.1 us (1%)
    all_to_all x2, blocking collectives, sum_columns(): return lax.all_to_all(chunks, ('zl', 'x'), 0, 0, tiled=True)  44.4 us
    all_to_all x4, blocking collectives, fan(): return lax.all_to_all(v, axis, 0, 0, tiled=True)  40.1 us
    all_gather x3, blocking collectives, pairs(): lax.all_gather(v, axis, axis=0, tiled=True, axis_index_groups=[[1, 2], [0...  32 us
    all_gather x3, blocking collectives, pairs(): lax.all_gather(v, axis, axis=0, tiled=True, axis_index_groups=[[0, 1], [2...  27 us
    ppermute x3, starting transfers between devices, gather_rows(): other = lax.ppermute(own, 'core', [(0, 1), (1, 0)])  5.73 us
    all_to_all x1, starting transfers between devices, fan(): return lax.all_to_all(v, axis, 0, 0, tiled=True)  4.71 us
    all_to_all x1, waiting for transfers between devices, fan(): return lax.all_to_all(v, axis, 0, 0, tiled=True)  4.69 us
    ppermute x3, waiting for transfers between devices, gather_rows(): other = lax.ppermute(own, 'core', [(0, 1), (1, 0)])  4.33 us
  transfers between devices with their start and end apart: 4, of which 4 were waited for; matrix products, arithmetic and copies ran while one was open for 0% of the time, Pallas kernels for 1%

commit v1 on v0

--- a/solution.py
+++ b/solution.py
@@ -88,6 +88,7 @@
 def tile_kernel(core, count, rows, cols, own, other, tiles, start, out):
     nout = out.shape[0]
     nsource = own.shape[0]
+    capacity = tiles.shape[0]
     live_count = count[0]
     mine = core[0]
     if start is None:
@@ -95,22 +96,29 @@
     else:
         out[...] = start[...]
 
+    width = min(unroll, capacity)
+
     def group(g, carry):
         terms = []
-        for u in range(unroll):
-            slot = g * unroll + u
+        for u in range(width):
+            slot = g * width + u
             live = slot < live_count
-            target = jnp.clip(cols[slot], 0, 2 * nsource - 1)
-            index = (target // 4) * 2 + target % 2
-            same = (target // 2) % 2 == mine
+            target = cols[slot] & (2 * nsource - 1)
+            index = ((target >> 2) << 1) | (target & 1)
+            same = ((target >> 1) & 1) == mine
             x = jnp.where(same, own[index], other[index])
             x = jnp.where(live, x, 0.0)
-            terms.append((jnp.clip(rows[slot], 0, nout - 1), product(x, tiles[slot])))
+            terms.append((rows[slot] & (nout - 1), product(x, tiles[slot])))
         for row, term in terms:
             out[row] = out[row] + term
         return carry
 
-    lax.fori_loop(0, (live_count + unroll - 1) // unroll, group, 0)
+    group(0, 0)
+    if capacity > width:
+
+        @pl.when(live_count > width)
+        def _():
+            group(1, 0)
 
 
 def vmem(n):

time: 175 us -> 173 us (0.989)
  no operation moved by 1% of the time
where the time goes in v1:
time: 173 us; the launch traced here: 171 us
  blocking collectives  143 us (83%)
  starting transfers between devices  9.77 us (6%)
  waiting for transfers between devices  9.01 us (5%)
  Pallas kernels  6.74 us (4%)
  between operations  2.11 us (1%)
    all_to_all x2, blocking collectives, sum_columns(): return lax.all_to_all(chunks, ('zl', 'x'), 0, 0, tiled=True)  43.4 us
    all_to_all x4, blocking collectives, fan(): return lax.all_to_all(v, axis, 0, 0, tiled=True)  40.2 us
    all_gather x3, blocking collectives, pairs(): lax.all_gather(v, axis, axis=0, tiled=True, axis_index_groups=[[1, 2], [0...  32 us
    all_gather x3, blocking collectives, pairs(): lax.all_gather(v, axis, axis=0, tiled=True, axis_index_groups=[[0, 1], [2...  27 us
    ppermute x3, starting transfers between devices, gather_rows(): other = lax.ppermute(own, 'core', [(0, 1), (1, 0)])  5.73 us
    all_to_all x1, waiting for transfers between devices, fan(): return lax.all_to_all(v, axis, 0, 0, tiled=True)  4.69 us
    ppermute x3, waiting for transfers between devices, gather_rows(): other = lax.ppermute(own, 'core', [(0, 1), (1, 0)])  4.33 us
    all_to_all x1, starting transfers between devices, fan(): return lax.all_to_all(v, axis, 0, 0, tiled=True)  4.04 us
  transfers between devices with their start and end apart: 4, of which 4 were waited for; matrix products, arithmetic and copies ran while one was open for 0% of the time, Pallas kernels for 1%

profile of v1, /device:TPU:24, one launch (start us, length us, event | category | flops | bytes accessed | tf_op | source)
XLA Modules:
  0.0 171.2 jit_solution(11767535356566947729)
XLA Ops:
  0.6 0.0 copy-start.4
  0.6 0.0 copy-start.5
  0.7 0.0 copy-start
  0.7 1.2 first.1
  1.9 9.7 %all-gather = f32[4,32,128]{2,1,0:T(8,128)S(1)} all-gather(f32[2,32,128]{2,1,0:T(8,128)S(1)} %first.1), channel_id=2, replica_groups={{0,32},{64,96},{1,33},{65,97},{2,34},{66,98},{3,35},{67,99},{4,36},{68,..., dimensions={0}, use_global_device_ids=true | all-gather | bytes 98304 | tf_op jit(solution)/shard_map/all_gather | solution.py:160
  11.6 14.0 %all_gather.19 = f32[4,2,32,128]{3,2,1,0:T(8,128)S(1)} all-gather(f32[2,2,32,128]{3,2,1,0:T(8,128)S(1)} %bitcast.51), channel_id=1, replica_groups={{32,64},{0,96},{33,65},{1,97},{34,66},{2,98},{35,67},{3,99},{36,68},{4,..., dimensions={0}, use_global_device_ids=true | all-gather | bytes 196608 | tf_op jit(solution)/shard_map/all_gather | solution.py:162
  25.7 10.5 %all_to_all.35 = f32[4,4,2,32,128]{4,3,2,1,0:T(8,128)S(1)} all-to-all(f32[4,4,2,32,128]{4,3,2,1,0:T(8,128)S(1)} %broadcast_in_dim.23), channel_id=1, replica_groups=mesh['y'=4,'zh'=4,'core'=2,'zl'=4,'x'=4] {'y'}, dimensions={0} | all-to-all | bytes 1048576 | tf_op jit(solution)/shard_map/all_to_all | solution.py:168
  36.2 1.9 %collective-permute-start = (f32[32,32,128]{2,1,0:T(8,128)S(1)}, f32[32,32,128]{2,1,0:T(8,128)S(1)}, u32[]{:S(2)}, u32[]{:S(2)}) collective-permute-start(f32[32,32,128]{2,1,0:T(8,128)S(1)} %bitcast.29), channel_id=1, source_target_pairs={{0,16},{16,0},{1,17},{17,1},{2,18},{18,2},{3,19},{19,3},{4,20},{20... | collective-permute-start | bytes 1572872 | tf_op jit(solution)/shard_map/ppermute | solution.py:175
  38.8 1.2 collective-permute-done.other
  40.0 0.0 copy-done.4
  40.0 0.0 copy-done.5
  40.0 0.0 copy-done
  40.0 0.0 copy-start.2
  40.0 0.0 copy-start.3
  40.0 1.2 shard_map.139
  41.2 23.4 %all_to_all.36.parts = f32[16,2,32,128]{3,2,1,0:T(8,128)S(1)} all-to-all(f32[16,2,32,128]{3,2,1,0:T(8,128)S(1)} %bitcast.36), channel_id=1, replica_groups=mesh['y'=4,'zh'=4,'core'=2,'zl'=4,'x'=4] {'zl','x'}, dimensions={0} | all-to-all | bytes 1048576 | tf_op jit(solution)/shard_map/all_to_all | solution.py:181
  64.6 0.0 copy-done.2
  64.6 0.0 copy-done.3
  64.6 0.2 shard_map.140.value
  64.8 8.6 %all-gather.1 = f32[4,32,128]{2,1,0:T(8,128)S(1)} all-gather(f32[2,32,128]{2,1,0:T(8,128)S(1)} %shard_map.140.value), channel_id=3, replica_groups={{0,32},{64,96},{1,33},{65,97},{2,34},{66,98},{3,35},{67,99},{4,36},{68,..., dimensions={0}, use_global_device_ids=true | all-gather | bytes 98304 | tf_op jit(solution)/shard_map/all_gather | solution.py:160
  73.4 9.0 %all_gather.21 = f32[4,2,32,128]{3,2,1,0:T(8,128)S(1)} all-gather(f32[2,2,32,128]{3,2,1,0:T(8,128)S(1)} %bitcast.52), channel_id=1, replica_groups={{32,64},{0,96},{33,65},{1,97},{34,66},{2,98},{35,67},{3,99},{36,68},{4,..., dimensions={0}, use_global_device_ids=true | all-gather | bytes 196608 | tf_op jit(solution)/shard_map/all_gather | solution.py:162
  82.5 10.5 %all_to_all.37 = f32[4,4,2,32,128]{4,3,2,1,0:T(8,128)S(1)} all-to-all(f32[4,4,2,32,128]{4,3,2,1,0:T(8,128)S(1)} %broadcast_in_dim.52), channel_id=1, replica_groups=mesh['y'=4,'zh'=4,'core'=2,'zl'=4,'x'=4] {'y'}, dimensions={0} | all-to-all | bytes 1048576 | tf_op jit(solution)/shard_map/all_to_all | solution.py:168
  93.0 1.9 %collective-permute-start.1 = (f32[32,32,128]{2,1,0:T(8,128)S(1)}, f32[32,32,128]{2,1,0:T(8,128)S(1)}, u32[]{:S(2)}, u32[]{:S(2)}) collective-permute-start(f32[32,32,128]{2,1,0:T(8,128)S(1)} %bitcast.33), channel_id=1, source_target_pairs={{0,16},{16,0},{1,17},{17,1},{2,18},{18,2},{3,19},{19,3},{4,20},{20... | collective-permute-start | bytes 1572872 | tf_op jit(solution)/shard_map/ppermute | solution.py:175
  94.9 1.9 %collective-permute-done.1.other = f32[32,32,128]{2,1,0:T(8,128)S(1)} collective-permute-done((f32[32,32,128]{2,1,0:T(8,128)S(1)}, f32[32,32,128]{2,1,0:T(8,128)S(1)}, u32[]{:S(2)}, u32[]{:S(2)}) %collective-permute-start.1) | collective-permute-done | bytes 524320 | tf_op jit(solution)/shard_map/ppermute | solution.py:175
  96.8 0.0 copy-start.6
  96.8 0.0 copy-start.7
  96.8 1.2 shard_map.142
  98.0 0.0 copy-start.1
  98.0 0.0 copy-start.8
  98.0 0.0 copy-start.9
  98.0 20.0 %all_to_all.38.parts = f32[16,2,32,128]{3,2,1,0:T(8,128)S(1)} all-to-all(f32[16,2,32,128]{3,2,1,0:T(8,128)S(1)} %bitcast.35), channel_id=1, replica_groups=mesh['y'=4,'zh'=4,'core'=2,'zl'=4,'x'=4] {'zl','x'}, dimensions={0} | all-to-all | bytes 1048576 | tf_op jit(solution)/shard_map/all_to_all | solution.py:181
  118.0 0.0 copy-done.6
  118.0 0.0 copy-done.7
  118.0 0.2 shard_map.143
  118.2 8.6 %all-gather.2 = f32[4,32,128]{2,1,0:T(8,128)S(1)} all-gather(f32[2,32,128]{2,1,0:T(8,128)S(1)} %get-tuple-element.5.value), channel_id=4, replica_groups={{0,32},{64,96},{1,33},{65,97},{2,34},{66,98},{3,35},{67,99},{4,36},{68,..., dimensions={0}, use_global_device_ids=true | all-gather | bytes 98304 | tf_op jit(solution)/shard_map/all_gather | solution.py:160
  126.9 9.0 %all_gather.23 = f32[4,2,32,128]{3,2,1,0:T(8,128)S(1)} all-gather(f32[2,2,32,128]{3,2,1,0:T(8,128)S(1)} %bitcast.53), channel_id=1, replica_groups={{32,64},{0,96},{33,65},{1,97},{34,66},{2,98},{35,67},{3,99},{36,68},{4,..., dimensions={0}, use_global_device_ids=true | all-gather | bytes 196608 | tf_op jit(solution)/shard_map/all_gather | solution.py:162
  135.9 10.6 %all_to_all.39 = f32[4,4,2,32,128]{4,3,2,1,0:T(8,128)S(1)} all-to-all(f32[4,4,2,32,128]{4,3,2,1,0:T(8,128)S(1)} %broadcast_in_dim.55), channel_id=1, replica_groups=mesh['y'=4,'zh'=4,'core'=2,'zl'=4,'x'=4] {'y'}, dimensions={0} | all-to-all | bytes 1048576 | tf_op jit(solution)/shard_map/all_to_all | solution.py:168
  146.5 1.9 %collective-permute-start.2 = (f32[32,32,128]{2,1,0:T(8,128)S(1)}, f32[32,32,128]{2,1,0:T(8,128)S(1)}, u32[]{:S(2)}, u32[]{:S(2)}) collective-permute-start(f32[32,32,128]{2,1,0:T(8,128)S(1)} %bitcast.31), channel_id=1, source_target_pairs={{0,16},{16,0},{1,17},{17,1},{2,18},{18,2},{3,19},{19,3},{4,20},{20... | collective-permute-start | bytes 1572872 | tf_op jit(solution)/shard_map/ppermute | solution.py:175
  149.1 1.2 collective-permute-done.2.other
  150.3 0.0 copy-done.1
  150.3 0.0 copy-done.8
  150.3 0.0 copy-done.9
  150.3 0.9 shard_map.145
  151.2 8.7 %all_to_all.40.parts = f32[4,2,32,128]{3,2,1,0:T(8,128)S(1)} all-to-all(f32[4,2,32,128]{3,2,1,0:T(8,128)S(1)} %broadcast_in_dim.56), channel_id=1, replica_groups=mesh['y'=4,'zh'=4,'core'=2,'zl'=4,'x'=4] {'x'}, dimensions={0} | all-to-all | bytes 262144 | tf_op jit(solution)/shard_map/all_to_all | solution.py:168
  159.9 0.7 broadcast_in_dim.57
  160.6 4.0 %all-to-all-start.6 = ((f32[4,2,32,128]{3,2,1,0:T(8,128)}), f32[4,2,32,128]{3,2,1,0:T(8,128)S(1)}, u32[]{:S(2)}, u32[]{:S(2)}) async-start(f32[4,2,32,128]{3,2,1,0:T(8,128)} %broadcast_in_dim.57), calls=%async_computation.6 | async-start | bytes 262144 | tf_op jit(solution)/shard_map/all_to_all | solution.py:168
  164.6 0.6 shard_map.141
  165.2 0.6 shard_map.144
  165.9 4.7 %all-to-all-done.6.parts = f32[4,2,32,128]{3,2,1,0:T(8,128)S(1)} async-done(((f32[4,2,32,128]{3,2,1,0:T(8,128)}), f32[4,2,32,128]{3,2,1,0:T(8,128)S(1)}, u32[]{:S(2)}, u32[]{:S(2)}) %all-to-all-start.6) | async-done | bytes 131104 | tf_op jit(solution)/shard_map/all_to_all | solution.py:168
  170.5 0.6 shard_map.147
  (5 shorter events, 0.2 us)
Async XLA Ops:
  0.6 39.4 %copy-start.4 = (s32[1,1,32]{2,1,0:T(1,128)S(1)}, s32[1,1,32]{2,1,0:T(1,128)}, u32[]{:S(2)}) copy-start(s32[1,1,32]{2,1,0:T(1,128)} %param.15) | copy-start | bytes 388
  0.6 39.3 %copy-start.5 = (s32[1,1,32]{2,1,0:T(1,128)S(1)}, s32[1,1,32]{2,1,0:T(1,128)}, u32[]{:S(2)}) copy-start(s32[1,1,32]{2,1,0:T(1,128)} %param.16) | copy-start | bytes 388
  0.7 39.3 %copy-start = (f32[1,1,32,128,128]{4,3,2,1,0:T(8,128)S(1)}, f32[1,1,32,128,128]{4,3,2,1,0:T(8,128)}, u32[]{:S(2)}) copy-start(f32[1,1,32,128,128]{4,3,2,1,0:T(8,128)} %param.14) | copy-start | bytes 6291460
  36.2 3.8 %collective-permute-start = (f32[32,32,128]{2,1,0:T(8,128)S(1)}, f32[32,32,128]{2,1,0:T(8,128)S(1)}, u32[]{:S(2)}, u32[]{:S(2)}) collective-permute-start(f32[32,32,128]{2,1,0:T(8,128)S(1)} %bitcast.29), channel_id=1, source_target_pairs={{0,16},{16,0},{1,17},{17,1},{2,18},{18,2},{3,19},{19,3},{4,20},{20... | collective-permute-start | bytes 1572872 | tf_op jit(solution)/shard_map/ppermute | solution.py:175
  40.0 24.6 %copy-start.2 = (f32[1,1,2,128,128]{4,3,2,1,0:T(8,128)S(1)}, f32[1,1,2,128,128]{4,3,2,1,0:T(8,128)}, u32[]{:S(2)}) copy-start(f32[1,1,2,128,128]{4,3,2,1,0:T(8,128)} %param.13) | copy-start | bytes 393220
  40.0 24.6 %copy-start.3 = (f32[1,1,2,32,128]{4,3,2,1,0:T(8,128)S(1)}, f32[1,1,2,32,128]{4,3,2,1,0:T(8,128)}, u32[]{:S(2)}) copy-start(f32[1,1,2,32,128]{4,3,2,1,0:T(8,128)} %param.12) | copy-start | bytes 98308
  93.0 3.8 %collective-permute-start.1 = (f32[32,32,128]{2,1,0:T(8,128)S(1)}, f32[32,32,128]{2,1,0:T(8,128)S(1)}, u32[]{:S(2)}, u32[]{:S(2)}) collective-permute-start(f32[32,32,128]{2,1,0:T(8,128)S(1)} %bitcast.33), channel_id=1, source_target_pairs={{0,16},{16,0},{1,17},{17,1},{2,18},{18,2},{3,19},{19,3},{4,20},{20... | collective-permute-start | bytes 1572872 | tf_op jit(solution)/shard_map/ppermute | solution.py:175
  96.8 21.2 %copy-start.6 = (f32[1,1,2,128]{3,2,1,0:T(2,128)S(1)}, f32[1,1,2,128]{3,2,1,0:T(2,128)}, u32[]{:S(2)}) copy-start(f32[1,1,2,128]{3,2,1,0:T(2,128)} %param.22) | copy-start | bytes 3076
  96.8 21.2 %copy-start.7 = (s32[1,1,2,128]{3,2,1,0:T(2,128)S(1)}, s32[1,1,2,128]{3,2,1,0:T(2,128)}, u32[]{:S(2)}) copy-start(s32[1,1,2,128]{3,2,1,0:T(2,128)} %param.23) | copy-start | bytes 3076
  98.0 52.3 %copy-start.1 = (f32[1,1,16,128,128]{4,3,2,1,0:T(8,128)S(1)}, f32[1,1,16,128,128]{4,3,2,1,0:T(8,128)}, u32[]{:S(2)}) copy-start(f32[1,1,16,128,128]{4,3,2,1,0:T(8,128)} %param.18) | copy-start | bytes 3145732
  98.0 52.3 %copy-start.8 = (s32[1,1,16]{2,1,0:T(1,128)S(1)}, s32[1,1,16]{2,1,0:T(1,128)}, u32[]{:S(2)}) copy-start(s32[1,1,16]{2,1,0:T(1,128)} %param.19) | copy-start | bytes 196
  98.0 52.3 %copy-start.9 = (s32[1,1,16]{2,1,0:T(1,128)S(1)}, s32[1,1,16]{2,1,0:T(1,128)}, u32[]{:S(2)}) copy-start(s32[1,1,16]{2,1,0:T(1,128)} %param.20) | copy-start | bytes 196
  146.5 3.8 %collective-permute-start.2 = (f32[32,32,128]{2,1,0:T(8,128)S(1)}, f32[32,32,128]{2,1,0:T(8,128)S(1)}, u32[]{:S(2)}, u32[]{:S(2)}) collective-permute-start(f32[32,32,128]{2,1,0:T(8,128)S(1)} %bitcast.31), channel_id=1, source_target_pairs={{0,16},{16,0},{1,17},{17,1},{2,18},{18,2},{3,19},{19,3},{4,20},{20... | collective-permute-start | bytes 1572872 | tf_op jit(solution)/shard_map/ppermute | solution.py:175
  160.6 10.0 %all-to-all-start.6 = ((f32[4,2,32,128]{3,2,1,0:T(8,128)}), f32[4,2,32,128]{3,2,1,0:T(8,128)S(1)}, u32[]{:S(2)}, u32[]{:S(2)}) async-start(f32[4,2,32,128]{3,2,1,0:T(8,128)} %broadcast_in_dim.57), calls=%async_computation.6 | async-start | bytes 262144 | tf_op jit(solution)/shard_map/all_to_all | solution.py:168

commit v2 on v1

--- a/solution.py
+++ b/solution.py
@@ -28,15 +28,20 @@
 
 
 def first_kernel(source_in, inverse_in, first, source, inverse, done):
-    arrivals = [
-        pltpu.make_async_copy(inverse_in, inverse, done.at[0]),
-        pltpu.make_async_copy(source_in, source, done.at[1]),
-    ]
-    for arrival in arrivals:
-        arrival.start()
-    for arrival in arrivals:
-        arrival.wait()
+    arrivals = []
     for p in range(source.shape[0]):
+        arrivals.append(
+            (
+                pltpu.make_async_copy(inverse_in.at[p], inverse.at[p], done.at[2 * p]),
+                pltpu.make_async_copy(source_in.at[p], source.at[p], done.at[2 * p + 1]),
+            )
+        )
+    for pair in arrivals:
+        for arrival in pair:
+            arrival.start()
+    for p in range(source.shape[0]):
+        for arrival in arrivals[p]:
+            arrival.wait()
         first[p] = omega * product(source[p], inverse[p])
 
 
@@ -214,7 +219,7 @@
         scratch_shapes=[
             pltpu.VMEM(block, f32),
             pltpu.VMEM(inverse.shape, f32),
-            pltpu.SemaphoreType.DMA((2,)),
+            pltpu.SemaphoreType.DMA((2 * block[0],)),
         ],
         compiler_params=pltpu.CompilerParams(vmem_limit_bytes=grant),
         name="first",

time: 173 us -> 172 us (level)
  no operation moved by 1% of the time
where the time goes in v2:
time: 172 us; the launch traced here: 170 us
  blocking collectives  142 us (83%)
  starting transfers between devices  9.77 us (6%)
  waiting for transfers between devices  9.01 us (5%)
  Pallas kernels  6.84 us (4%)
  between operations  2.11 us (1%)
    all_to_all x2, blocking collectives, sum_columns(): return lax.all_to_all(chunks, ('zl', 'x'), 0, 0, tiled=True)  42.5 us
    all_to_all x4, blocking collectives, fan(): return lax.all_to_all(v, axis, 0, 0, tiled=True)  40.2 us
    all_gather x3, blocking collectives, pairs(): lax.all_gather(v, axis, axis=0, tiled=True, axis_index_groups=[[1, 2], [0...  32.1 us
    all_gather x3, blocking collectives, pairs(): lax.all_gather(v, axis, axis=0, tiled=True, axis_index_groups=[[0, 1], [2...  27 us
    ppermute x3, starting transfers between devices, gather_rows(): other = lax.ppermute(own, 'core', [(0, 1), (1, 0)])  5.73 us
    all_to_all x1, waiting for transfers between devices, fan(): return lax.all_to_all(v, axis, 0, 0, tiled=True)  4.69 us
    ppermute x3, waiting for transfers between devices, gather_rows(): other = lax.ppermute(own, 'core', [(0, 1), (1, 0)])  4.33 us
    all_to_all x1, starting transfers between devices, fan(): return lax.all_to_all(v, axis, 0, 0, tiled=True)  4.04 us
  transfers between devices with their start and end apart: 4, of which 4 were waited for; matrix products, arithmetic and copies ran while one was open for 0% of the time, Pallas kernels for 1%

profile of v2, /device:TPU:24, one launch (start us, length us, event | category | flops | bytes accessed | tf_op | source)
XLA Modules:
  0.0 170.3 jit_solution(9334805556976072633)
XLA Ops:
  0.6 0.0 copy-start.4
  0.6 0.0 copy-start.5
  0.7 0.0 copy-start
  0.7 1.3 first.1
  2.0 9.7 %all-gather = f32[4,32,128]{2,1,0:T(8,128)S(1)} all-gather(f32[2,32,128]{2,1,0:T(8,128)S(1)} %first.1), channel_id=2, replica_groups={{0,32},{64,96},{1,33},{65,97},{2,34},{66,98},{3,35},{67,99},{4,36},{68,..., dimensions={0}, use_global_device_ids=true | all-gather | bytes 98304 | tf_op jit(solution)/shard_map/all_gather | solution.py:165
  11.7 14.0 %all_gather.19 = f32[4,2,32,128]{3,2,1,0:T(8,128)S(1)} all-gather(f32[2,2,32,128]{3,2,1,0:T(8,128)S(1)} %bitcast.51), channel_id=1, replica_groups={{32,64},{0,96},{33,65},{1,97},{34,66},{2,98},{35,67},{3,99},{36,68},{4,..., dimensions={0}, use_global_device_ids=true | all-gather | bytes 196608 | tf_op jit(solution)/shard_map/all_gather | solution.py:167
  25.8 10.5 %all_to_all.35 = f32[4,4,2,32,128]{4,3,2,1,0:T(8,128)S(1)} all-to-all(f32[4,4,2,32,128]{4,3,2,1,0:T(8,128)S(1)} %broadcast_in_dim.23), channel_id=1, replica_groups=mesh['y'=4,'zh'=4,'core'=2,'zl'=4,'x'=4] {'y'}, dimensions={0} | all-to-all | bytes 1048576 | tf_op jit(solution)/shard_map/all_to_all | solution.py:173
  36.3 1.9 %collective-permute-start = (f32[32,32,128]{2,1,0:T(8,128)S(1)}, f32[32,32,128]{2,1,0:T(8,128)S(1)}, u32[]{:S(2)}, u32[]{:S(2)}) collective-permute-start(f32[32,32,128]{2,1,0:T(8,128)S(1)} %bitcast.29), channel_id=1, source_target_pairs={{0,16},{16,0},{1,17},{17,1},{2,18},{18,2},{3,19},{19,3},{4,20},{20... | collective-permute-start | bytes 1572872 | tf_op jit(solution)/shard_map/ppermute | solution.py:180
  38.9 1.2 collective-permute-done.other
  40.1 0.0 copy-done.4
  40.1 0.0 copy-done.5
  40.1 0.0 copy-done
  40.1 0.0 copy-start.2
  40.1 0.0 copy-start.3
  40.1 1.2 shard_map.139
  41.3 22.5 %all_to_all.36.parts = f32[16,2,32,128]{3,2,1,0:T(8,128)S(1)} all-to-all(f32[16,2,32,128]{3,2,1,0:T(8,128)S(1)} %bitcast.36), channel_id=1, replica_groups=mesh['y'=4,'zh'=4,'core'=2,'zl'=4,'x'=4] {'zl','x'}, dimensions={0} | all-to-all | bytes 1048576 | tf_op jit(solution)/shard_map/all_to_all | solution.py:186
  63.8 0.0 copy-done.2
  63.8 0.0 copy-done.3
  63.8 0.2 shard_map.140.value
  64.0 8.6 %all-gather.1 = f32[4,32,128]{2,1,0:T(8,128)S(1)} all-gather(f32[2,32,128]{2,1,0:T(8,128)S(1)} %shard_map.140.value), channel_id=3, replica_groups={{0,32},{64,96},{1,33},{65,97},{2,34},{66,98},{3,35},{67,99},{4,36},{68,..., dimensions={0}, use_global_device_ids=true | all-gather | bytes 98304 | tf_op jit(solution)/shard_map/all_gather | solution.py:165
  72.6 9.0 %all_gather.21 = f32[4,2,32,128]{3,2,1,0:T(8,128)S(1)} all-gather(f32[2,2,32,128]{3,2,1,0:T(8,128)S(1)} %bitcast.52), channel_id=1, replica_groups={{32,64},{0,96},{33,65},{1,97},{34,66},{2,98},{35,67},{3,99},{36,68},{4,..., dimensions={0}, use_global_device_ids=true | all-gather | bytes 196608 | tf_op jit(solution)/shard_map/all_gather | solution.py:167
  81.7 10.4 %all_to_all.37 = f32[4,4,2,32,128]{4,3,2,1,0:T(8,128)S(1)} all-to-all(f32[4,4,2,32,128]{4,3,2,1,0:T(8,128)S(1)} %broadcast_in_dim.52), channel_id=1, replica_groups=mesh['y'=4,'zh'=4,'core'=2,'zl'=4,'x'=4] {'y'}, dimensions={0} | all-to-all | bytes 1048576 | tf_op jit(solution)/shard_map/all_to_all | solution.py:173
  92.1 1.9 %collective-permute-start.1 = (f32[32,32,128]{2,1,0:T(8,128)S(1)}, f32[32,32,128]{2,1,0:T(8,128)S(1)}, u32[]{:S(2)}, u32[]{:S(2)}) collective-permute-start(f32[32,32,128]{2,1,0:T(8,128)S(1)} %bitcast.33), channel_id=1, source_target_pairs={{0,16},{16,0},{1,17},{17,1},{2,18},{18,2},{3,19},{19,3},{4,20},{20... | collective-permute-start | bytes 1572872 | tf_op jit(solution)/shard_map/ppermute | solution.py:180
  94.0 1.9 %collective-permute-done.1.other = f32[32,32,128]{2,1,0:T(8,128)S(1)} collective-permute-done((f32[32,32,128]{2,1,0:T(8,128)S(1)}, f32[32,32,128]{2,1,0:T(8,128)S(1)}, u32[]{:S(2)}, u32[]{:S(2)}) %collective-permute-start.1) | collective-permute-done | bytes 524320 | tf_op jit(solution)/shard_map/ppermute | solution.py:180
  95.9 0.0 copy-start.6
  95.9 0.0 copy-start.7
  95.9 1.2 shard_map.142
  97.1 0.0 copy-start.1
  97.2 0.0 copy-start.8
  97.2 0.0 copy-start.9
  97.2 20.0 %all_to_all.38.parts = f32[16,2,32,128]{3,2,1,0:T(8,128)S(1)} all-to-all(f32[16,2,32,128]{3,2,1,0:T(8,128)S(1)} %bitcast.35), channel_id=1, replica_groups=mesh['y'=4,'zh'=4,'core'=2,'zl'=4,'x'=4] {'zl','x'}, dimensions={0} | all-to-all | bytes 1048576 | tf_op jit(solution)/shard_map/all_to_all | solution.py:186
  117.2 0.0 copy-done.6
  117.2 0.0 copy-done.7
  117.2 0.2 shard_map.143
  117.4 8.6 %all-gather.2 = f32[4,32,128]{2,1,0:T(8,128)S(1)} all-gather(f32[2,32,128]{2,1,0:T(8,128)S(1)} %get-tuple-element.5.value), channel_id=4, replica_groups={{0,32},{64,96},{1,33},{65,97},{2,34},{66,98},{3,35},{67,99},{4,36},{68,..., dimensions={0}, use_global_device_ids=true | all-gather | bytes 98304 | tf_op jit(solution)/shard_map/all_gather | solution.py:165
  126.0 9.0 %all_gather.23 = f32[4,2,32,128]{3,2,1,0:T(8,128)S(1)} all-gather(f32[2,2,32,128]{3,2,1,0:T(8,128)S(1)} %bitcast.53), channel_id=1, replica_groups={{32,64},{0,96},{33,65},{1,97},{34,66},{2,98},{35,67},{3,99},{36,68},{4,..., dimensions={0}, use_global_device_ids=true | all-gather | bytes 196608 | tf_op jit(solution)/shard_map/all_gather | solution.py:167
  135.1 10.6 %all_to_all.39 = f32[4,4,2,32,128]{4,3,2,1,0:T(8,128)S(1)} all-to-all(f32[4,4,2,32,128]{4,3,2,1,0:T(8,128)S(1)} %broadcast_in_dim.55), channel_id=1, replica_groups=mesh['y'=4,'zh'=4,'core'=2,'zl'=4,'x'=4] {'y'}, dimensions={0} | all-to-all | bytes 1048576 | tf_op jit(solution)/shard_map/all_to_all | solution.py:173
  145.7 1.9 %collective-permute-start.2 = (f32[32,32,128]{2,1,0:T(8,128)S(1)}, f32[32,32,128]{2,1,0:T(8,128)S(1)}, u32[]{:S(2)}, u32[]{:S(2)}) collective-permute-start(f32[32,32,128]{2,1,0:T(8,128)S(1)} %bitcast.31), channel_id=1, source_target_pairs={{0,16},{16,0},{1,17},{17,1},{2,18},{18,2},{3,19},{19,3},{4,20},{20... | collective-permute-start | bytes 1572872 | tf_op jit(solution)/shard_map/ppermute | solution.py:180
  148.2 1.2 collective-permute-done.2.other
  149.5 0.0 copy-done.1
  149.5 0.0 copy-done.8
  149.5 0.0 copy-done.9
  149.5 0.9 shard_map.145
  150.4 8.7 %all_to_all.40.parts = f32[4,2,32,128]{3,2,1,0:T(8,128)S(1)} all-to-all(f32[4,2,32,128]{3,2,1,0:T(8,128)S(1)} %broadcast_in_dim.56), channel_id=1, replica_groups=mesh['y'=4,'zh'=4,'core'=2,'zl'=4,'x'=4] {'x'}, dimensions={0} | all-to-all | bytes 262144 | tf_op jit(solution)/shard_map/all_to_all | solution.py:173
  159.0 0.7 broadcast_in_dim.57
  159.7 4.0 %all-to-all-start.6 = ((f32[4,2,32,128]{3,2,1,0:T(8,128)}), f32[4,2,32,128]{3,2,1,0:T(8,128)S(1)}, u32[]{:S(2)}, u32[]{:S(2)}) async-start(f32[4,2,32,128]{3,2,1,0:T(8,128)} %broadcast_in_dim.57), calls=%async_computation.6 | async-start | bytes 262144 | tf_op jit(solution)/shard_map/all_to_all | solution.py:173
  163.8 0.6 shard_map.141
  164.4 0.6 shard_map.144
  165.0 4.7 %all-to-all-done.6.parts = f32[4,2,32,128]{3,2,1,0:T(8,128)S(1)} async-done(((f32[4,2,32,128]{3,2,1,0:T(8,128)}), f32[4,2,32,128]{3,2,1,0:T(8,128)S(1)}, u32[]{:S(2)}, u32[]{:S(2)}) %all-to-all-start.6) | async-done | bytes 131104 | tf_op jit(solution)/shard_map/all_to_all | solution.py:173
  169.7 0.6 shard_map.147
  (5 shorter events, 0.2 us)
Async XLA Ops:
  0.6 39.5 %copy-start.4 = (s32[1,1,32]{2,1,0:T(1,128)S(1)}, s32[1,1,32]{2,1,0:T(1,128)}, u32[]{:S(2)}) copy-start(s32[1,1,32]{2,1,0:T(1,128)} %param.15) | copy-start | bytes 388
  0.6 39.4 %copy-start.5 = (s32[1,1,32]{2,1,0:T(1,128)S(1)}, s32[1,1,32]{2,1,0:T(1,128)}, u32[]{:S(2)}) copy-start(s32[1,1,32]{2,1,0:T(1,128)} %param.16) | copy-start | bytes 388
  0.7 39.4 %copy-start = (f32[1,1,32,128,128]{4,3,2,1,0:T(8,128)S(1)}, f32[1,1,32,128,128]{4,3,2,1,0:T(8,128)}, u32[]{:S(2)}) copy-start(f32[1,1,32,128,128]{4,3,2,1,0:T(8,128)} %param.14) | copy-start | bytes 6291460
  36.3 3.8 %collective-permute-start = (f32[32,32,128]{2,1,0:T(8,128)S(1)}, f32[32,32,128]{2,1,0:T(8,128)S(1)}, u32[]{:S(2)}, u32[]{:S(2)}) collective-permute-start(f32[32,32,128]{2,1,0:T(8,128)S(1)} %bitcast.29), channel_id=1, source_target_pairs={{0,16},{16,0},{1,17},{17,1},{2,18},{18,2},{3,19},{19,3},{4,20},{20... | collective-permute-start | bytes 1572872 | tf_op jit(solution)/shard_map/ppermute | solution.py:180
  40.1 23.7 %copy-start.2 = (f32[1,1,2,128,128]{4,3,2,1,0:T(8,128)S(1)}, f32[1,1,2,128,128]{4,3,2,1,0:T(8,128)}, u32[]{:S(2)}) copy-start(f32[1,1,2,128,128]{4,3,2,1,0:T(8,128)} %param.13) | copy-start | bytes 393220
  40.1 23.7 %copy-start.3 = (f32[1,1,2,32,128]{4,3,2,1,0:T(8,128)S(1)}, f32[1,1,2,32,128]{4,3,2,1,0:T(8,128)}, u32[]{:S(2)}) copy-start(f32[1,1,2,32,128]{4,3,2,1,0:T(8,128)} %param.12) | copy-start | bytes 98308
  92.1 3.8 %collective-permute-start.1 = (f32[32,32,128]{2,1,0:T(8,128)S(1)}, f32[32,32,128]{2,1,0:T(8,128)S(1)}, u32[]{:S(2)}, u32[]{:S(2)}) collective-permute-start(f32[32,32,128]{2,1,0:T(8,128)S(1)} %bitcast.33), channel_id=1, source_target_pairs={{0,16},{16,0},{1,17},{17,1},{2,18},{18,2},{3,19},{19,3},{4,20},{20... | collective-permute-start | bytes 1572872 | tf_op jit(solution)/shard_map/ppermute | solution.py:180
  95.9 21.2 %copy-start.6 = (f32[1,1,2,128]{3,2,1,0:T(2,128)S(1)}, f32[1,1,2,128]{3,2,1,0:T(2,128)}, u32[]{:S(2)}) copy-start(f32[1,1,2,128]{3,2,1,0:T(2,128)} %param.22) | copy-start | bytes 3076
  95.9 21.2 %copy-start.7 = (s32[1,1,2,128]{3,2,1,0:T(2,128)S(1)}, s32[1,1,2,128]{3,2,1,0:T(2,128)}, u32[]{:S(2)}) copy-start(s32[1,1,2,128]{3,2,1,0:T(2,128)} %param.23) | copy-start | bytes 3076
  97.1 52.3 %copy-start.1 = (f32[1,1,16,128,128]{4,3,2,1,0:T(8,128)S(1)}, f32[1,1,16,128,128]{4,3,2,1,0:T(8,128)}, u32[]{:S(2)}) copy-start(f32[1,1,16,128,128]{4,3,2,1,0:T(8,128)} %param.18) | copy-start | bytes 3145732
  97.2 52.3 %copy-start.8 = (s32[1,1,16]{2,1,0:T(1,128)S(1)}, s32[1,1,16]{2,1,0:T(1,128)}, u32[]{:S(2)}) copy-start(s32[1,1,16]{2,1,0:T(1,128)} %param.19) | copy-start | bytes 196
  97.2 52.3 %copy-start.9 = (s32[1,1,16]{2,1,0:T(1,128)S(1)}, s32[1,1,16]{2,1,0:T(1,128)}, u32[]{:S(2)}) copy-start(s32[1,1,16]{2,1,0:T(1,128)} %param.20) | copy-start | bytes 196
  145.7 3.8 %collective-permute-start.2 = (f32[32,32,128]{2,1,0:T(8,128)S(1)}, f32[32,32,128]{2,1,0:T(8,128)S(1)}, u32[]{:S(2)}, u32[]{:S(2)}) collective-permute-start(f32[32,32,128]{2,1,0:T(8,128)S(1)} %bitcast.31), channel_id=1, source_target_pairs={{0,16},{16,0},{1,17},{17,1},{2,18},{18,2},{3,19},{19,3},{4,20},{20... | collective-permute-start | bytes 1572872 | tf_op jit(solution)/shard_map/ppermute | solution.py:180
  159.7 10.0 %all-to-all-start.6 = ((f32[4,2,32,128]{3,2,1,0:T(8,128)}), f32[4,2,32,128]{3,2,1,0:T(8,128)S(1)}, u32[]{:S(2)}, u32[]{:S(2)}) async-start(f32[4,2,32,128]{3,2,1,0:T(8,128)} %broadcast_in_dim.57), calls=%async_computation.6 | async-start | bytes 262144 | tf_op jit(solution)/shard_map/all_to_all | solution.py:173

commit v3 on v2

--- a/solution.py
+++ b/solution.py
@@ -109,7 +109,8 @@
             slot = g * width + u
             live = slot < live_count
             target = cols[slot] & (2 * nsource - 1)
-            index = ((target >> 2) << 1) | (target & 1)
+            plane = (0x78 >> (2 * ((target >> 2) & 3))) & 3
+            index = ((target >> 4) << 3) | (plane << 1) | (target & 1)
             same = ((target >> 1) & 1) == mine
             x = jnp.where(same, own[index], other[index])
             x = jnp.where(live, x, 0.0)
@@ -162,9 +163,9 @@
 
 
 def pairs(v, axis):
-    v = lax.all_gather(v, axis, axis=0, tiled=True, axis_index_groups=[[0, 1], [2, 3]])
+    v = lax.all_gather(v, axis, axis=0, tiled=True, axis_index_groups=[[1, 2], [0, 3]])
     v = lax.optimization_barrier(v)
-    return lax.all_gather(v, axis, axis=0, tiled=True, axis_index_groups=[[1, 2], [0, 3]])
+    return lax.all_gather(v, axis, axis=0, tiled=True, axis_index_groups=[[0, 1], [3, 2]])
 
 
 def fan(v, axis):

time: 172 us -> 173 us (level)
    all_to_all x4, blocking collectives: 40.2 us -> 42.5 us  [fan(): return lax.all_to_all(v, axis, 0, 0, tiled=True)]
    all_to_all x2, blocking collectives: 42.5 us -> 40.4 us  [sum_columns(): return lax.all_to_all(chunks, ('zl', 'x'), 0, 0, tiled=True)]
where the time goes in v3:
time: 173 us; the launch traced here: 171 us
  blocking collectives  143 us (83%)
  starting transfers between devices  9.05 us (5%)
  waiting for transfers between devices  8.98 us (5%)
  Pallas kernels  6.84 us (4%)
  between operations  2.12 us (1%)
    all_to_all x4, blocking collectives, fan(): return lax.all_to_all(v, axis, 0, 0, tiled=True)  42.5 us
    all_to_all x2, blocking collectives, sum_columns(): return lax.all_to_all(chunks, ('zl', 'x'), 0, 0, tiled=True)  40.4 us
    all_gather x3, blocking collectives, pairs(): lax.all_gather(v, axis, axis=0, tiled=True, axis_index_groups=[[1, 2], [0...  32.4 us
    all_gather x3, blocking collectives, pairs(): lax.all_gather(v, axis, axis=0, tiled=True, axis_index_groups=[[0, 1], [3...  28.1 us
    ppermute x3, starting transfers between devices, gather_rows(): other = lax.ppermute(own, 'core', [(0, 1), (1, 0)])  5.73 us
    all_to_all x1, waiting for transfers between devices, fan(): return lax.all_to_all(v, axis, 0, 0, tiled=True)  4.65 us
    ppermute x3, waiting for transfers between devices, gather_rows(): other = lax.ppermute(own, 'core', [(0, 1), (1, 0)])  4.33 us
  transfers between devices with their start and end apart: 4, of which 4 were waited for; matrix products, arithmetic and copies ran while one was open for 0% of the time, Pallas kernels for 1%

profile of v3, /device:TPU:24, one launch (start us, length us, event | category | flops | bytes accessed | tf_op | source)
XLA Modules:
  0.0 171.3 jit_solution(8698657154953224428)
XLA Ops:
  0.6 0.0 copy-start.4
  0.6 0.0 copy-start.5
  0.7 0.0 copy-start
  0.7 1.3 first.1
  2.0 14.1 %all-gather = f32[4,32,128]{2,1,0:T(8,128)S(1)} all-gather(f32[2,32,128]{2,1,0:T(8,128)S(1)} %first.1), channel_id=2, replica_groups={{32,64},{0,96},{33,65},{1,97},{34,66},{2,98},{35,67},{3,99},{36,68},{4,..., dimensions={0}, use_global_device_ids=true | all-gather | bytes 98304 | tf_op jit(solution)/shard_map/all_gather | solution.py:166
  16.1 10.4 %all_gather.19 = f32[4,2,32,128]{3,2,1,0:T(8,128)S(1)} all-gather(f32[2,2,32,128]{3,2,1,0:T(8,128)S(1)} %bitcast.51), channel_id=1, replica_groups={{0,32},{96,64},{1,33},{97,65},{2,34},{98,66},{3,35},{99,67},{4,36},{100..., dimensions={0}, use_global_device_ids=true | all-gather | bytes 196608 | tf_op jit(solution)/shard_map/all_gather | solution.py:168
  26.6 11.0 %all_to_all.35 = f32[4,4,2,32,128]{4,3,2,1,0:T(8,128)S(1)} all-to-all(f32[4,4,2,32,128]{4,3,2,1,0:T(8,128)S(1)} %broadcast_in_dim.23), channel_id=1, replica_groups=mesh['y'=4,'zh'=4,'core'=2,'zl'=4,'x'=4] {'y'}, dimensions={0} | all-to-all | bytes 1048576 | tf_op jit(solution)/shard_map/all_to_all | solution.py:174
  37.6 1.9 %collective-permute-start = (f32[32,32,128]{2,1,0:T(8,128)S(1)}, f32[32,32,128]{2,1,0:T(8,128)S(1)}, u32[]{:S(2)}, u32[]{:S(2)}) collective-permute-start(f32[32,32,128]{2,1,0:T(8,128)S(1)} %bitcast.29), channel_id=1, source_target_pairs={{0,16},{16,0},{1,17},{17,1},{2,18},{18,2},{3,19},{19,3},{4,20},{20... | collective-permute-start | bytes 1572872 | tf_op jit(solution)/shard_map/ppermute | solution.py:181
  40.1 1.2 collective-permute-done.other
  41.4 0.0 copy-done.4
  41.4 0.0 copy-done.5
  41.4 0.0 copy-done
  41.4 0.0 copy-start.2
  41.4 0.0 copy-start.3
  41.4 1.2 shard_map.139
  42.6 20.3 %all_to_all.36.parts = f32[16,2,32,128]{3,2,1,0:T(8,128)S(1)} all-to-all(f32[16,2,32,128]{3,2,1,0:T(8,128)S(1)} %bitcast.36), channel_id=1, replica_groups=mesh['y'=4,'zh'=4,'core'=2,'zl'=4,'x'=4] {'zl','x'}, dimensions={0} | all-to-all | bytes 1048576 | tf_op jit(solution)/shard_map/all_to_all | solution.py:187
  62.9 0.0 copy-done.2
  62.9 0.0 copy-done.3
  62.9 0.2 shard_map.140.value
  63.1 9.6 %all-gather.1 = f32[4,32,128]{2,1,0:T(8,128)S(1)} all-gather(f32[2,32,128]{2,1,0:T(8,128)S(1)} %shard_map.140.value), channel_id=3, replica_groups={{32,64},{0,96},{33,65},{1,97},{34,66},{2,98},{35,67},{3,99},{36,68},{4,..., dimensions={0}, use_global_device_ids=true | all-gather | bytes 98304 | tf_op jit(solution)/shard_map/all_gather | solution.py:166
  72.7 8.8 %all_gather.21 = f32[4,2,32,128]{3,2,1,0:T(8,128)S(1)} all-gather(f32[2,2,32,128]{3,2,1,0:T(8,128)S(1)} %bitcast.52), channel_id=1, replica_groups={{0,32},{96,64},{1,33},{97,65},{2,34},{98,66},{3,35},{99,67},{4,36},{100..., dimensions={0}, use_global_device_ids=true | all-gather | bytes 196608 | tf_op jit(solution)/shard_map/all_gather | solution.py:168
  81.6 10.8 %all_to_all.37 = f32[4,4,2,32,128]{4,3,2,1,0:T(8,128)S(1)} all-to-all(f32[4,4,2,32,128]{4,3,2,1,0:T(8,128)S(1)} %broadcast_in_dim.52), channel_id=1, replica_groups=mesh['y'=4,'zh'=4,'core'=2,'zl'=4,'x'=4] {'y'}, dimensions={0} | all-to-all | bytes 1048576 | tf_op jit(solution)/shard_map/all_to_all | solution.py:174
  92.3 1.9 %collective-permute-start.1 = (f32[32,32,128]{2,1,0:T(8,128)S(1)}, f32[32,32,128]{2,1,0:T(8,128)S(1)}, u32[]{:S(2)}, u32[]{:S(2)}) collective-permute-start(f32[32,32,128]{2,1,0:T(8,128)S(1)} %bitcast.33), channel_id=1, source_target_pairs={{0,16},{16,0},{1,17},{17,1},{2,18},{18,2},{3,19},{19,3},{4,20},{20... | collective-permute-start | bytes 1572872 | tf_op jit(solution)/shard_map/ppermute | solution.py:181
  94.3 1.9 %collective-permute-done.1.other = f32[32,32,128]{2,1,0:T(8,128)S(1)} collective-permute-done((f32[32,32,128]{2,1,0:T(8,128)S(1)}, f32[32,32,128]{2,1,0:T(8,128)S(1)}, u32[]{:S(2)}, u32[]{:S(2)}) %collective-permute-start.1) | collective-permute-done | bytes 524320 | tf_op jit(solution)/shard_map/ppermute | solution.py:181
  96.1 0.0 copy-start.6
  96.1 0.0 copy-start.7
  96.1 1.2 shard_map.142
  97.3 0.0 copy-start.1
  97.4 0.0 copy-start.8
  97.4 0.0 copy-start.9
  97.4 20.1 %all_to_all.38.parts = f32[16,2,32,128]{3,2,1,0:T(8,128)S(1)} all-to-all(f32[16,2,32,128]{3,2,1,0:T(8,128)S(1)} %bitcast.35), channel_id=1, replica_groups=mesh['y'=4,'zh'=4,'core'=2,'zl'=4,'x'=4] {'zl','x'}, dimensions={0} | all-to-all | bytes 1048576 | tf_op jit(solution)/shard_map/all_to_all | solution.py:187
  117.5 0.0 copy-done.6
  117.5 0.0 copy-done.7
  117.5 0.2 shard_map.143
  117.7 8.7 %all-gather.2 = f32[4,32,128]{2,1,0:T(8,128)S(1)} all-gather(f32[2,32,128]{2,1,0:T(8,128)S(1)} %get-tuple-element.5.value), channel_id=4, replica_groups={{32,64},{0,96},{33,65},{1,97},{34,66},{2,98},{35,67},{3,99},{36,68},{4,..., dimensions={0}, use_global_device_ids=true | all-gather | bytes 98304 | tf_op jit(solution)/shard_map/all_gather | solution.py:166
  126.4 8.8 %all_gather.23 = f32[4,2,32,128]{3,2,1,0:T(8,128)S(1)} all-gather(f32[2,2,32,128]{3,2,1,0:T(8,128)S(1)} %bitcast.53), channel_id=1, replica_groups={{0,32},{96,64},{1,33},{97,65},{2,34},{98,66},{3,35},{99,67},{4,36},{100..., dimensions={0}, use_global_device_ids=true | all-gather | bytes 196608 | tf_op jit(solution)/shard_map/all_gather | solution.py:168
  135.3 10.5 %all_to_all.39 = f32[4,4,2,32,128]{4,3,2,1,0:T(8,128)S(1)} all-to-all(f32[4,4,2,32,128]{4,3,2,1,0:T(8,128)S(1)} %broadcast_in_dim.55), channel_id=1, replica_groups=mesh['y'=4,'zh'=4,'core'=2,'zl'=4,'x'=4] {'y'}, dimensions={0} | all-to-all | bytes 1048576 | tf_op jit(solution)/shard_map/all_to_all | solution.py:174
  145.8 1.9 %collective-permute-start.2 = (f32[32,32,128]{2,1,0:T(8,128)S(1)}, f32[32,32,128]{2,1,0:T(8,128)S(1)}, u32[]{:S(2)}, u32[]{:S(2)}) collective-permute-start(f32[32,32,128]{2,1,0:T(8,128)S(1)} %bitcast.31), channel_id=1, source_target_pairs={{0,16},{16,0},{1,17},{17,1},{2,18},{18,2},{3,19},{19,3},{4,20},{20... | collective-permute-start | bytes 1572872 | tf_op jit(solution)/shard_map/ppermute | solution.py:181
  148.3 1.2 collective-permute-done.2.other
  149.6 0.0 copy-done.1
  149.6 0.0 copy-done.8
  149.6 0.0 copy-done.9
  149.6 0.9 shard_map.145
  150.5 10.3 %all_to_all.40.parts = f32[4,2,32,128]{3,2,1,0:T(8,128)S(1)} all-to-all(f32[4,2,32,128]{3,2,1,0:T(8,128)S(1)} %broadcast_in_dim.56), channel_id=1, replica_groups=mesh['y'=4,'zh'=4,'core'=2,'zl'=4,'x'=4] {'x'}, dimensions={0} | all-to-all | bytes 262144 | tf_op jit(solution)/shard_map/all_to_all | solution.py:174
  160.8 0.7 broadcast_in_dim.57
  161.4 3.3 %all-to-all-start.6 = ((f32[4,2,32,128]{3,2,1,0:T(8,128)}), f32[4,2,32,128]{3,2,1,0:T(8,128)S(1)}, u32[]{:S(2)}, u32[]{:S(2)}) async-start(f32[4,2,32,128]{3,2,1,0:T(8,128)} %broadcast_in_dim.57), calls=%async_computation.6 | async-start | bytes 262144 | tf_op jit(solution)/shard_map/all_to_all | solution.py:174
  164.8 0.6 shard_map.141
  165.4 0.6 shard_map.144
  166.0 4.7 %all-to-all-done.6.parts = f32[4,2,32,128]{3,2,1,0:T(8,128)S(1)} async-done(((f32[4,2,32,128]{3,2,1,0:T(8,128)}), f32[4,2,32,128]{3,2,1,0:T(8,128)S(1)}, u32[]{:S(2)}, u32[]{:S(2)}) %all-to-all-start.6) | async-done | bytes 131104 | tf_op jit(solution)/shard_map/all_to_all | solution.py:174
  170.7 0.6 shard_map.147
  (5 shorter events, 0.2 us)
Async XLA Ops:
  0.6 40.7 %copy-start.4 = (s32[1,1,32]{2,1,0:T(1,128)S(1)}, s32[1,1,32]{2,1,0:T(1,128)}, u32[]{:S(2)}) copy-start(s32[1,1,32]{2,1,0:T(1,128)} %param.15) | copy-start | bytes 388
  0.6 40.7 %copy-start.5 = (s32[1,1,32]{2,1,0:T(1,128)S(1)}, s32[1,1,32]{2,1,0:T(1,128)}, u32[]{:S(2)}) copy-start(s32[1,1,32]{2,1,0:T(1,128)} %param.16) | copy-start | bytes 388
  0.7 40.7 %copy-start = (f32[1,1,32,128,128]{4,3,2,1,0:T(8,128)S(1)}, f32[1,1,32,128,128]{4,3,2,1,0:T(8,128)}, u32[]{:S(2)}) copy-start(f32[1,1,32,128,128]{4,3,2,1,0:T(8,128)} %param.14) | copy-start | bytes 6291460
  37.6 3.8 %collective-permute-start = (f32[32,32,128]{2,1,0:T(8,128)S(1)}, f32[32,32,128]{2,1,0:T(8,128)S(1)}, u32[]{:S(2)}, u32[]{:S(2)}) collective-permute-start(f32[32,32,128]{2,1,0:T(8,128)S(1)} %bitcast.29), channel_id=1, source_target_pairs={{0,16},{16,0},{1,17},{17,1},{2,18},{18,2},{3,19},{19,3},{4,20},{20... | collective-permute-start | bytes 1572872 | tf_op jit(solution)/shard_map/ppermute | solution.py:181
  41.4 21.5 %copy-start.2 = (f32[1,1,2,128,128]{4,3,2,1,0:T(8,128)S(1)}, f32[1,1,2,128,128]{4,3,2,1,0:T(8,128)}, u32[]{:S(2)}) copy-start(f32[1,1,2,128,128]{4,3,2,1,0:T(8,128)} %param.13) | copy-start | bytes 393220
  41.4 21.5 %copy-start.3 = (f32[1,1,2,32,128]{4,3,2,1,0:T(8,128)S(1)}, f32[1,1,2,32,128]{4,3,2,1,0:T(8,128)}, u32[]{:S(2)}) copy-start(f32[1,1,2,32,128]{4,3,2,1,0:T(8,128)} %param.12) | copy-start | bytes 98308
  92.3 3.8 %collective-permute-start.1 = (f32[32,32,128]{2,1,0:T(8,128)S(1)}, f32[32,32,128]{2,1,0:T(8,128)S(1)}, u32[]{:S(2)}, u32[]{:S(2)}) collective-permute-start(f32[32,32,128]{2,1,0:T(8,128)S(1)} %bitcast.33), channel_id=1, source_target_pairs={{0,16},{16,0},{1,17},{17,1},{2,18},{18,2},{3,19},{19,3},{4,20},{20... | collective-permute-start | bytes 1572872 | tf_op jit(solution)/shard_map/ppermute | solution.py:181
  96.1 21.4 %copy-start.6 = (f32[1,1,2,128]{3,2,1,0:T(2,128)S(1)}, f32[1,1,2,128]{3,2,1,0:T(2,128)}, u32[]{:S(2)}) copy-start(f32[1,1,2,128]{3,2,1,0:T(2,128)} %param.22) | copy-start | bytes 3076
  96.1 21.4 %copy-start.7 = (s32[1,1,2,128]{3,2,1,0:T(2,128)S(1)}, s32[1,1,2,128]{3,2,1,0:T(2,128)}, u32[]{:S(2)}) copy-start(s32[1,1,2,128]{3,2,1,0:T(2,128)} %param.23) | copy-start | bytes 3076
  97.3 52.2 %copy-start.1 = (f32[1,1,16,128,128]{4,3,2,1,0:T(8,128)S(1)}, f32[1,1,16,128,128]{4,3,2,1,0:T(8,128)}, u32[]{:S(2)}) copy-start(f32[1,1,16,128,128]{4,3,2,1,0:T(8,128)} %param.18) | copy-start | bytes 3145732
  97.4 52.2 %copy-start.8 = (s32[1,1,16]{2,1,0:T(1,128)S(1)}, s32[1,1,16]{2,1,0:T(1,128)}, u32[]{:S(2)}) copy-start(s32[1,1,16]{2,1,0:T(1,128)} %param.19) | copy-start | bytes 196
  97.4 52.2 %copy-start.9 = (s32[1,1,16]{2,1,0:T(1,128)S(1)}, s32[1,1,16]{2,1,0:T(1,128)}, u32[]{:S(2)}) copy-start(s32[1,1,16]{2,1,0:T(1,128)} %param.20) | copy-start | bytes 196
  145.8 3.8 %collective-permute-start.2 = (f32[32,32,128]{2,1,0:T(8,128)S(1)}, f32[32,32,128]{2,1,0:T(8,128)S(1)}, u32[]{:S(2)}, u32[]{:S(2)}) collective-permute-start(f32[32,32,128]{2,1,0:T(8,128)S(1)} %bitcast.31), channel_id=1, source_target_pairs={{0,16},{16,0},{1,17},{17,1},{2,18},{18,2},{3,19},{19,3},{4,20},{20... | collective-permute-start | bytes 1572872 | tf_op jit(solution)/shard_map/ppermute | solution.py:181
  161.4 9.2 %all-to-all-start.6 = ((f32[4,2,32,128]{3,2,1,0:T(8,128)}), f32[4,2,32,128]{3,2,1,0:T(8,128)S(1)}, u32[]{:S(2)}, u32[]{:S(2)}) async-start(f32[4,2,32,128]{3,2,1,0:T(8,128)} %broadcast_in_dim.57), calls=%async_computation.6 | async-start | bytes 262144 | tf_op jit(solution)/shard_map/all_to_all | solution.py:174
